TPU v7x, 32 devices: a whole 2x2x4 slice. The times are simulated.
32 devices in a mesh: expert: 8 (over z, x), dp: 4 (over y, core).
Axes of the slice: x: 2, y: 2, z: 4, core: 2. Of those that a mesh axis runs over, the one named last changes fastest.
Arguments:
- enc_state: bfloat16 [4, 8, 256, 1024], P('dp', 'expert'), may hold values from -6 to 6
- baseline: bfloat16 [4, 8, 256, 1024], P('dp', 'expert'), may hold values from -6 to 6
- enc_keys: bfloat16 [4, 8, 256, 1024], P('dp', 'expert'), may hold values from -4 to 4
- dec_queries: bfloat16 [4, 8, 128, 1024], P('dp', 'expert'), may hold values from -200 to 200
- out_mult: bfloat16 [4, 8, 128, 1024], P('dp', 'expert'), may hold values from -6 to 6
- doc_lengths: int32 [4, 8], P('dp', 'expert'), may hold values from 128 to 256, as said below
- expert_ids: int32 [4, 8, 256], P('dp', 'expert'), may hold values from 0 to 15
- slot_ids: int32 [4, 8, 256], P('dp', 'expert'), may hold values from 0 to 31, as said below
- gate_prob: float32 [4, 8, 256], P('dp', 'expert'), may hold values from 0.2 to 1
- norm_gain: float32 [1024], replicated, may hold values from 0.5 to 2
- w_in: bfloat16 [16, 1024, 2816], P('expert', None, 'dp'), may hold values from -0.1875 to 0.1875
- w_out_t: bfloat16 [16, 1024, 2816], P('expert', None, 'dp'), may hold values from -0.109375 to 0.109375
- w_value: bfloat16 [1024, 1024], replicated, may hold values from -0.1875 to 0.1875
Outputs:
- enc_mult: bfloat16 [4, 8, 256, 1024], P('dp', 'expert')
Inputs may be any that keep to these rules, and one draw needn't show every extreme that they name: `slot_ids`: within one document no two tokens share an expert and a slot, and every token has a slot; one expert has all 32 slots used in every document. `doc_lengths`: some document has all 256 tokens.
All inputs are finite; a program needn't handle non-finite values.
Results may differ from a plain program's by a relative error of at most 0.0069.
Values may be sent and summed in bfloat16 or wider, within the bound.
A program may use at most 128 MiB of HBM per device.

v0:
```python
import math
import jax
import jax.numpy as jnp
from jax import lax
from jax.sharding import PartitionSpec as P

HEADS = 16
HEAD_DIM = 64


def rescale(pre_act, base_act):
    upper_part = jnp.maximum(jnp.maximum(pre_act, base_act), 0.0)
    lower_part = jnp.maximum(-jnp.minimum(pre_act, base_act), 0.0)
    return upper_part / (upper_part + lower_part + jnp.where(upper_part > 0.0, 0.0, 1.0))


def attend(query_rows, key_rows, mult_rows, length, w_value):
    enc_len = key_rows.shape[0]
    dec_len = query_rows.shape[0]
    queries = query_rows.reshape(dec_len, HEADS, HEAD_DIM)
    keys = key_rows.reshape(enc_len, HEADS, HEAD_DIM)
    mults = mult_rows.reshape(dec_len, HEADS, HEAD_DIM)
    scores = jnp.einsum("qhd,khd->hqk", queries, keys, preferred_element_type=jnp.float32) * (
        1.0 / math.sqrt(HEAD_DIM)
    )
    valid = jnp.arange(enc_len, dtype=jnp.int32) < length
    scores = jnp.where(valid[None, None, :], scores, -jnp.inf)
    top_score = jnp.max(scores, axis=-1, keepdims=True)
    expo = jnp.exp(scores - top_score)
    attn = (expo / jnp.sum(expo, axis=-1, keepdims=True)).astype(jnp.bfloat16)
    value_mult = jnp.einsum("hqk,qhd->khd", attn, mults, preferred_element_type=jnp.float32).astype(
        jnp.bfloat16
    )
    return lax.dot_general(
        value_mult.reshape(enc_len, HEADS * HEAD_DIM),
        w_value,
        (((1,), (1,)), ((), ())),
        preferred_element_type=jnp.float32,
    )


def expert_terms(rows_in, rows_base, rows_mult, part_in, part_out):
    pre_act = jnp.einsum("erd,edf->erf", rows_in, part_in, preferred_element_type=jnp.float32)
    base_act = jnp.einsum("erd,edf->erf", rows_base, part_in, preferred_element_type=jnp.float32)
    hidden_mult = jnp.einsum(
        "erd,edf->erf", rows_mult, part_out, preferred_element_type=jnp.float32
    )
    act_mult = (rescale(pre_act, base_act) * hidden_mult).astype(jnp.bfloat16)
    return jnp.einsum("erf,edf->erd", act_mult, part_in, preferred_element_type=jnp.float32)


def body(
    enc_state,
    baseline,
    enc_keys,
    dec_queries,
    out_mult,
    doc_lengths,
    expert_ids,
    slot_ids,
    gate_prob,
    norm_gain,
    w_in,
    w_out_t,
    w_value,
):
    enc_len = enc_state.shape[2]
    feature_width = enc_state.shape[3]
    local_experts = w_in.shape[0]
    n_experts = local_experts * lax.axis_size("expert")
    capacity = max(2, 2 * enc_len // n_experts)
    tokens = enc_state[0, 0].astype(jnp.float32)
    row_scale = norm_gain * lax.rsqrt(jnp.mean(tokens * tokens, axis=-1, keepdims=True) + 1e-06)
    inputs = (tokens * row_scale).astype(jnp.bfloat16)
    base_inputs = (baseline[0, 0].astype(jnp.float32) * row_scale).astype(jnp.bfloat16)
    flat_slot = expert_ids[0, 0] * capacity + slot_ids[0, 0]
    onehot = (
        flat_slot[None, :] == jnp.arange(n_experts * capacity, dtype=jnp.int32)[:, None]
    ).astype(jnp.bfloat16)

    def dispatch(values):
        placed = jnp.dot(onehot, values, preferred_element_type=jnp.float32).astype(jnp.bfloat16)
        return placed.reshape(n_experts, capacity, feature_width)

    layer_mult = attend(
        dec_queries[0, 0], enc_keys[0, 0], out_mult[0, 0], doc_lengths[0, 0], w_value
    )
    scaled_mult = (gate_prob[0, 0][:, None] * layer_mult).astype(jnp.bfloat16)
    sent_in, sent_base, sent_mult = (
        lax.all_to_all(dispatch(inputs), "expert", split_axis=0, concat_axis=1, tiled=True),
        lax.all_to_all(dispatch(base_inputs), "expert", split_axis=0, concat_axis=1, tiled=True),
        lax.all_to_all(dispatch(scaled_mult), "expert", split_axis=0, concat_axis=1, tiled=True),
    )
    slot_mult = expert_terms(
        sent_in,
        sent_base,
        sent_mult,
        lax.all_gather(w_in, "dp", axis=2, tiled=True),
        lax.all_gather(w_out_t, "dp", axis=2, tiled=True),
    )
    returned = lax.all_to_all(
        slot_mult.astype(jnp.bfloat16), "expert", split_axis=1, concat_axis=0, tiled=True
    )
    per_token = lax.dot_general(
        onehot,
        returned.reshape(n_experts * capacity, feature_width),
        (((0,), (0,)), ((), ())),
        preferred_element_type=jnp.float32,
    )
    result = (layer_mult + row_scale * per_token).astype(jnp.bfloat16)
    return result[None, None]


def solution(mesh):
    in_specs = (
        P("dp", "expert", None, None),
        P("dp", "expert", None, None),
        P("dp", "expert", None, None),
        P("dp", "expert", None, None),
        P("dp", "expert", None, None),
        P("dp", "expert"),
        P("dp", "expert", None),
        P("dp", "expert", None),
        P("dp", "expert", None),
        P(),
        P("expert", None, "dp"),
        P("expert", None, "dp"),
        P(),
    )
    out_specs = P("dp", "expert", None, None)
    return jax.shard_map(body, mesh=mesh, in_specs=in_specs, out_specs=out_specs, check_vma=False)
```

profile of v0, /device:TPU:0, one launch (start us, length us, event | category | flops | bytes accessed | tf_op | source)
XLA Modules:
  0.0 230.6 jit_solution(66276424766294604)
XLA Ops:
  6.5 0.0 copy-start
  6.5 0.0 copy-start.4
  6.5 0.0 copy-start.8
  6.5 0.0 copy-start.9
  6.5 0.0 all-gather.3.cloned.1.call-start
  6.6 0.7 all-gather.3.cloned.1.call-update
  7.3 0.0 copy-start.5
  7.3 0.0 all-gather.5.cloned.1.call-start
  7.3 0.7 all-gather.5.cloned.1.call-update
  8.0 0.0 copy-done.4
  8.1 0.2 fusion.5
  8.2 0.0 copy-done.8
  8.3 0.0 copy-done.9
  8.3 0.0 copy-done.6
  8.3 2.6 %convolution_convert_fusion.1 = bf16[512,1024]{1,0:T(8,128)(2,1)} fusion(bf16[1,1,256,1024]{3,2,1,0:T(8,128)(2,1)} %param.14, f32[256]{0:T(256)S(1)} %add_rsqrt_fusion, f32[1024]{0:T(1024)S(1)} %copy-done.6, s32[256]{0:T(256)S(1)} %bitcast.71), kind=kOutput, calls=%fused_computation.10 | convolution fusion | flops 270139392 | bytes 1579008 | tf_op jit(solution)/shard_map/dot_general | solution.py:82
  10.9 7.3 %all-to-all-start.1 = ((bf16[16,32,1024]{2,1,0:T(8,128)(2,1)}), bf16[16,32,1024]{2,1,0:T(8,128)(2,1)S(1)}, u32[]{:S(2)}, u32[]{:S(2)}) async-start(bf16[16,32,1024]{2,1,0:T(8,128)(2,1)} %bitcast.66), calls=%async_computation.1 | async-start | bytes 2097152 | tf_op jit(solution)/shard_map/all_to_all | solution.py:91
  18.2 2.6 %convolution_convert_fusion.2 = bf16[512,1024]{1,0:T(8,128)(2,1)} fusion(bf16[1,1,256,1024]{3,2,1,0:T(8,128)(2,1)} %param.13, f32[256]{0:T(256)S(1)} %add_rsqrt_fusion, f32[1024]{0:T(1024)S(1)} %copy-done.6, s32[256]{0:T(256)S(1)} %bitcast.72), kind=kOutput, calls=%fused_computation.11 | convolution fusion | flops 270139392 | bytes 1579008 | tf_op jit(solution)/shard_map/dot_general | solution.py:82
  20.8 23.1 %all-to-all-done.1 = bf16[16,32,1024]{2,1,0:T(8,128)(2,1)S(1)} async-done(((bf16[16,32,1024]{2,1,0:T(8,128)(2,1)}), bf16[16,32,1024]{2,1,0:T(8,128)(2,1)S(1)}, u32[]{:S(2)}, u32[]{:S(2)}) %all-to-all-start.1) | async-done | bytes 1048608 | tf_op jit(solution)/shard_map/all_to_all | solution.py:91
  44.0 4.2 %all-to-all-start = ((bf16[16,32,1024]{2,1,0:T(8,128)(2,1)}), bf16[16,32,1024]{2,1,0:T(8,128)(2,1)}, u32[]{:S(2)}, u32[]{:S(2)}) async-start(bf16[16,32,1024]{2,1,0:T(8,128)(2,1)} %bitcast.62), calls=%async_computation | async-start | bytes 2097152 | tf_op jit(solution)/shard_map/all_to_all | solution.py:90
  48.9 0.0 copy-done.5
  48.9 0.8 copy.39
  49.7 1.1 copy.41
  50.8 2.0 copy.40
  52.9 3.2 %fusion.28 = (f32[16,128]{1,0:T(8,128)S(1)}, f32[16,128,256]{2,1,0:T(8,128)}) fusion(pred[256]{0:T(512)(128)(4,1)S(1)} %iota_compare_fusion.5, bf16[128,16,64]{0,2,1:T(8,128)(2,1)} %bitcast.70, bf16[256,16,64]{0,2,1:T(8,128)(2,1)} %bitcast.68), kind=kOutput, calls=%fused_computation.43 | convolution fusion | flops 69206272 | bytes 2892032 | tf_op jit(solution)/shard_map/sub | solution.py:29
  56.0 2.2 convolution_convert_fusion.4
  58.2 0.0 copy-done.2
  58.3 0.0 copy-done
  58.3 0.8 fusion.29
  59.0 0.0 copy-done.7
  59.1 1.5 convolution_convert_fusion
  60.6 13.2 %all-to-all-done = bf16[16,32,1024]{2,1,0:T(8,128)(2,1)} async-done(((bf16[16,32,1024]{2,1,0:T(8,128)(2,1)}), bf16[16,32,1024]{2,1,0:T(8,128)(2,1)}, u32[]{:S(2)}, u32[]{:S(2)}) %all-to-all-start) | async-done | bytes 1048608 | tf_op jit(solution)/shard_map/all_to_all | solution.py:90
  73.8 3.7 %all-to-all-start.2 = ((bf16[16,32,1024]{2,1,0:T(8,128)(2,1)}), bf16[16,32,1024]{2,1,0:T(8,128)(2,1)S(1)}, u32[]{:S(2)}, u32[]{:S(2)}) async-start(bf16[16,32,1024]{2,1,0:T(8,128)(2,1)} %bitcast.19), calls=%async_computation.2 | async-start | bytes 2097152 | tf_op jit(solution)/shard_map/all_to_all | solution.py:92
  77.5 1.3 copy.43
  78.8 2.4 %copy.42 = bf16[8,2,32,1024]{3,2,0,1:T(8,128)(2,1)} copy(bf16[8,2,32,1024]{3,2,1,0:T(8,128)(2,1)} %bitcast.10) | data formatting | bytes 2097152 | tf_op jit(solution)/shard_map/all_to_all | solution.py:90
  81.3 22.0 %all-to-all-done.2 = bf16[16,32,1024]{2,1,0:T(8,128)(2,1)S(1)} async-done(((bf16[16,32,1024]{2,1,0:T(8,128)(2,1)}), bf16[16,32,1024]{2,1,0:T(8,128)(2,1)S(1)}, u32[]{:S(2)}, u32[]{:S(2)}) %all-to-all-start.2) | async-done | bytes 1048608 | tf_op jit(solution)/shard_map/all_to_all | solution.py:92
  103.2 1.1 copy.44
  104.3 10.3 %fusion.30 = f32[2,256,2816]{2,1,0:T(8,128)} fusion(bf16[2,256,1024]{2,1,0:T(8,128)(2,1)} %bitcast.65, bf16[2,1024,2816]{1,2,0:T(8,128)(2,1)} %all-gather.3.cloned.1.call-done), kind=kOutput, calls=%fused_computation.45 | convolution fusion | flops 2952790016 | bytes 18350080 | tf_op jit(solution)/shard_map/erd,edf->erf/dot_general | solution.py:43
  114.6 13.8 %fusion.31 = f32[2,256,2816]{2,1,0:T(8,128)} fusion(bf16[2,256,1024]{2,1,0:T(8,128)(2,1)S(1)} %bitcast.63, bf16[2,1024,2816]{1,2,0:T(8,128)(2,1)} %all-gather.3.cloned.1.call-done), kind=kOutput, calls=%fused_computation.46 | convolution fusion | flops 2952790016 | bytes 18350080 | tf_op jit(solution)/shard_map/erd,edf->erf/dot_general | solution.py:44
  128.4 37.1 %all-gather.5.cloned.1.call-done = bf16[2,1024,2816]{1,2,0:T(8,128)(2,1)} async-done(((bf16[2,1024,704]{1,2,0:T(8,128)(2,1)}), bf16[2,1024,2816]{1,2,0:T(8,128)(2,1)}) %all-gather.5.cloned.1.call-update) | async-done | bytes 11534352 | tf_op jit(solution)/shard_map/all_gather | solution.py:99
  165.5 0.0 copy-done.3
  165.5 15.6 %multiply_convert_fusion = bf16[2,256,2816]{2,1,0:T(8,128)(2,1)} fusion(f32[2,256,2816]{2,1,0:T(8,128)} %fusion.30, f32[2,256,2816]{2,1,0:T(8,128)} %fusion.31, bf16[2,256,1024]{2,1,0:T(8,128)(2,1)S(1)} %bitcast.64, bf16[2,1024,2816]{1,2,0:T(8,128)(2,1)} %all-gather.5.cloned.1.call-done), kind=kOutput, calls=%fused_computation.1 | convolution fusion | flops 2970091520 | bytes 27000832 | tf_op jit(solution)/shard_map/erd,edf->erf/dot_general | solution.py:45
  181.1 8.4 %convolution_convert_fusion.3 = bf16[2,256,1024]{2,1,0:T(8,128)(2,1)S(1)} fusion(bf16[2,256,2816]{2,1,0:T(8,128)(2,1)} %multiply_convert_fusion, bf16[2,1024,2816]{1,2,0:T(8,128)(2,1)} %all-gather.3.cloned.1.call-done), kind=kOutput, calls=%fused_computation.12 | convolution fusion | flops 2953314304 | bytes 15466496 | tf_op jit(solution)/shard_map/erf,edf->erd/dot_general | solution.py:49
  189.5 1.1 copy.45
  190.6 31.4 %all_to_all.69 = bf16[2,256,1024]{2,0,1:T(2,128)(2,1)S(1)} all-to-all(bf16[2,256,1024]{2,0,1:T(2,128)(2,1)S(1)} %copy.45), channel_id=1, replica_groups=mesh['expert'=8,'dp'=4] {'expert'}, dimensions={1} | all-to-all | bytes 2097152 | tf_op jit(solution)/shard_map/all_to_all | solution.py:101
  222.1 0.3 copy.46
  222.3 0.1 copy.47
  222.4 1.3 fusion.4
  223.7 0.0 copy-done.1
  (9 shorter events, 0.0 us)
Async XLA Ops:
  6.5 51.7 %copy-start = (bf16[1024,1024]{1,0:T(8,128)(2,1)S(1)}, bf16[1024,1024]{1,0:T(8,128)(2,1)}, u32[]{:S(2)}) copy-start(bf16[1024,1024]{1,0:T(8,128)(2,1)} %param.25) | copy-start | bytes 6291460
  6.5 1.5 copy-start.4
  6.5 1.7 copy-start.8
  6.5 1.7 copy-start.9
  6.5 1.7 copy-start.6
  6.5 97.8 %all-gather.3.cloned.1.call-start = ((), (), s32[]{:S(2)}) async-start(), calls=%async_computation.4 | async-start | bytes 14417920 | tf_op jit(solution)/shard_map/all_gather | solution.py:98
  7.3 41.6 %copy-start.5 = (bf16[1,1,128,1024]{3,2,1,0:T(8,128)(2,1)S(1)}, bf16[1,1,128,1024]{3,2,1,0:T(8,128)(2,1)}, u32[]{:S(2)}) copy-start(bf16[1,1,128,1024]{3,2,1,0:T(8,128)(2,1)} %param.16) | copy-start | bytes 786436
  7.3 158.2 %all-gather.5.cloned.1.call-start = ((), (), s32[]{:S(2)}) async-start(), calls=%async_computation.5 | async-start | bytes 14417920 | tf_op jit(solution)/shard_map/all_gather | solution.py:99
  10.9 33.0 %all-to-all-start.1 = ((bf16[16,32,1024]{2,1,0:T(8,128)(2,1)}), bf16[16,32,1024]{2,1,0:T(8,128)(2,1)S(1)}, u32[]{:S(2)}, u32[]{:S(2)}) async-start(bf16[16,32,1024]{2,1,0:T(8,128)(2,1)} %bitcast.66), calls=%async_computation.1 | async-start | bytes 2097152 | tf_op jit(solution)/shard_map/all_to_all | solution.py:91
  44.0 14.3 %copy-start.2 = (bf16[16,32,1024]{2,1,0:T(8,128)(2,1)}, bf16[16,32,1024]{2,1,0:T(8,128)(2,1)S(1)}, u32[]{:S(2)}) copy-start(bf16[16,32,1024]{2,1,0:T(8,128)(2,1)S(1)} %all-to-all-done.1) | copy-start | bytes 3145732
  44.0 29.8 %all-to-all-start = ((bf16[16,32,1024]{2,1,0:T(8,128)(2,1)}), bf16[16,32,1024]{2,1,0:T(8,128)(2,1)}, u32[]{:S(2)}, u32[]{:S(2)}) async-start(bf16[16,32,1024]{2,1,0:T(8,128)(2,1)} %bitcast.62), calls=%async_computation | async-start | bytes 2097152 | tf_op jit(solution)/shard_map/all_to_all | solution.py:90
  56.0 3.0 %copy-start.7 = (f32[1,1,256]{2,1,0:T(1,128)S(1)}, f32[1,1,256]{2,1,0:T(1,128)}, u32[]{:S(2)}) copy-start(f32[1,1,256]{2,1,0:T(1,128)} %param.21) | copy-start | bytes 3076
  73.8 29.5 %all-to-all-start.2 = ((bf16[16,32,1024]{2,1,0:T(8,128)(2,1)}), bf16[16,32,1024]{2,1,0:T(8,128)(2,1)S(1)}, u32[]{:S(2)}, u32[]{:S(2)}) async-start(bf16[16,32,1024]{2,1,0:T(8,128)(2,1)} %bitcast.19), calls=%async_computation.2 | async-start | bytes 2097152 | tf_op jit(solution)/shard_map/all_to_all | solution.py:92
  114.6 50.9 %copy-start.3 = (bf16[2,8,32,1024]{3,2,1,0:T(8,128)(2,1)S(1)}, bf16[2,8,32,1024]{3,2,1,0:T(8,128)(2,1)}, u32[]{:S(2)}) copy-start(bf16[2,8,32,1024]{3,2,1,0:T(8,128)(2,1)} %copy.44) | copy-start | bytes 3145732
  181.1 42.6 %copy-start.1 = (bf16[1024,1024]{1,0:T(8,128)(2,1)S(1)}, bf16[1024,1024]{1,0:T(8,128)(2,1)}, u32[]{:S(2)}) copy-start(bf16[1024,1024]{1,0:T(8,128)(2,1)} %param.25) | copy-start | bytes 6291460
Sparse Core Ops, SparseCore 0:
  8.9 78.8 all-gather.2
  89.4 76.1 all-gather.4
where the time goes:
time: 231 us
  waiting for transfers between devices  96.8 us (42%)
  matrix products  62.3 us (27%)
  blocking collectives  31.4 us (14%)
  starting transfers between devices  15.3 us (7%)
  between operations  14.2 us (6%)
  local copies, waits for them, and re-layouts  10.3 us (4%)
    all_gather x1, waiting for transfers between devices, body(): lax.all_gather(w_out_t, 'dp', axis=2, tiled=True)  37.1 us
    all_to_all x1, blocking collectives, body(): lax.all_to_all(slot_mult.astype(jnp.bfloat16), 'expert', split_axis=1, co...  31.4 us
    all_to_all x1, waiting for transfers between devices, body(): lax.all_to_all(dispatch(base_inputs), 'expert', split_axis=0, concat_axis...  23.1 us
    all_to_all x1, waiting for transfers between devices, body(): lax.all_to_all(dispatch(scaled_mult), 'expert', split_axis=0, concat_axis...  22 us
    dot_general x1, matrix products, expert_terms(): jnp.einsum('erd,edf->erf', rows_mult, part_out, preferred_element_type=jn...  15.6 us
    dot_general x1, matrix products, expert_terms(): jnp.einsum('erd,edf->erf', rows_base, part_in, preferred_element_type=jnp...  13.8 us
    all_to_all x1, waiting for transfers between devices, body(): lax.all_to_all(dispatch(inputs), 'expert', split_axis=0, concat_axis=1, t...  13.2 us
    dot_general x1, matrix products, expert_terms(): jnp.einsum('erd,edf->erf', rows_in, part_in, preferred_element_type=jnp.f...  10.3 us
  transfers between devices with their start and end apart: 5, of which 4 were waited for; matrix products, arithmetic and copies ran while one was open for 20% of the time, Pallas kernels for 0%

commit v1 on v0

--- a/solution.py
+++ b/solution.py
@@ -88,7 +88,15 @@
     scaled_mult = (gate_prob[0, 0][:, None] * layer_mult).astype(jnp.bfloat16)
     sent_in, sent_base, sent_mult = (
         lax.all_to_all(dispatch(inputs), "expert", split_axis=0, concat_axis=1, tiled=True),
-        lax.all_to_all(dispatch(base_inputs), "expert", split_axis=0, concat_axis=1, tiled=True),
+        jnp.concatenate(
+            lax.all_to_all(
+                jnp.stack(jnp.split(dispatch(base_inputs), lax.axis_size("expert"), axis=0)),
+                "expert",
+                0,
+                0,
+            ),
+            axis=1,
+        ),
         lax.all_to_all(dispatch(scaled_mult), "expert", split_axis=0, concat_axis=1, tiled=True),
     )
     slot_mult = expert_terms(

time: 231 us -> 231 us (level)
  local copies, waits for them, and re-layouts: 10.3 us -> 15.6 us
  waiting for transfers between devices: 96.8 us -> 92.5 us
    unnamed x23 -> x30, local copies, waits for them, and re-layouts: 4.04 us -> 8.65 us
    all_gather x1, waiting for transfers between devices: 37.1 us -> 32.6 us  [body(): lax.all_gather(w_out_t, 'dp', axis=2, tiled=True)]
  transfers between devices with their start and end apart: 5 -> 5, of which waited for: 4 -> 4; matrix products, arithmetic and copies ran while one was open for 20% -> 22% of each run, Pallas kernels for 0% -> 0%
where the time goes in v1:
time: 231 us
  waiting for transfers between devices  92.5 us (40%)
  matrix products  61.3 us (27%)
  blocking collectives  31.4 us (14%)
  local copies, waits for them, and re-layouts  15.6 us (7%)
  starting transfers between devices  15.3 us (7%)
  between operations  14.2 us (6%)
    all_gather x1, waiting for transfers between devices, body(): lax.all_gather(w_out_t, 'dp', axis=2, tiled=True)  32.6 us
    all_to_all x1, blocking collectives, body(): lax.all_to_all(slot_mult.astype(jnp.bfloat16), 'expert', split_axis=1, co...  31.4 us
    all_to_all x1, waiting for transfers between devices, body(): lax.all_to_all(jnp.stack(jnp.split(dispatch(base_inputs), lax.axis_size('...  23.2 us
    all_to_all x1, waiting for transfers between devices, body(): lax.all_to_all(dispatch(scaled_mult), 'expert', split_axis=0, concat_axis...  22.1 us
    dot_general x1, matrix products, expert_terms(): jnp.einsum('erd,edf->erf', rows_mult, part_out, preferred_element_type=jn...  15.6 us
    dot_general x1, matrix products, expert_terms(): jnp.einsum('erd,edf->erf', rows_base, part_in, preferred_element_type=jnp...  13.7 us
    all_to_all x1, waiting for transfers between devices, body(): lax.all_to_all(dispatch(inputs), 'expert', split_axis=0, concat_axis=1, t...  13.3 us
    dot_general x1, matrix products, expert_terms(): jnp.einsum('erd,edf->erf', rows_in, part_in, preferred_element_type=jnp.f...  10.4 us
  transfers between devices with their start and end apart: 5, of which 4 were waited for; matrix products, arithmetic and copies ran while one was open for 22% of the time, Pallas kernels for 0%

profile of v1, /device:TPU:0, one launch (start us, length us, event | category | flops | bytes accessed | tf_op | source)
XLA Modules:
  0.0 230.6 jit_solution(638680258245271635)
XLA Ops:
  6.5 0.0 copy-start
  6.5 0.0 all-gather.3.cloned.1.call-start
  6.6 0.7 all-gather.3.cloned.1.call-update
  7.3 0.0 all-gather.5.cloned.1.call-start
  7.3 0.7 all-gather.5.cloned.1.call-update
  8.0 0.0 copy-done.4
  8.0 0.2 fusion.5
  8.2 0.0 copy-done.8
  8.2 0.0 copy-done.9
  8.3 0.0 copy-start.5
  8.3 1.6 convolution_convert_fusion.1
  9.9 0.1 fusion.28
  10.1 0.7 constant_dynamic-update-slice_fusion.7
  10.7 0.7 constant_dynamic-update-slice_fusion.6
  11.4 0.7 constant_dynamic-update-slice_fusion.5
  12.0 0.7 constant_dynamic-update-slice_fusion.4
  12.7 0.7 constant_dynamic-update-slice_fusion.3
  13.3 0.7 constant_dynamic-update-slice_fusion.2
  14.0 0.7 constant_dynamic-update-slice_fusion.1
  14.7 0.7 constant_dynamic-update-slice_fusion
  15.3 7.3 %all-to-all-start.1 = ((bf16[8,2,32,1024]{3,2,1,0:T(8,128)(2,1)}), bf16[8,2,32,1024]{3,2,1,0:T(8,128)(2,1)S(1)}, u32[]{:S(2)}, u32[]{:S(2)}) async-start(bf16[8,2,32,1024]{3,2,1,0:T(8,128)(2,1)} %constant_dynamic-update-slice_fusion), calls=%async_computation.1 | async-start | bytes 2097152 | tf_op jit(solution)/shard_map/all_to_all | solution.py:92
  22.6 2.6 %convolution_convert_fusion.2 = bf16[512,1024]{1,0:T(8,128)(2,1)} fusion(bf16[1,1,256,1024]{3,2,1,0:T(8,128)(2,1)} %param.13, f32[256]{0:T(256)S(1)} %add_rsqrt_fusion, f32[1024]{0:T(1024)S(1)} %copy-done.6, s32[256]{0:T(256)S(1)} %bitcast.84), kind=kOutput, calls=%fused_computation.11 | convolution fusion | flops 270139392 | bytes 1579008 | tf_op jit(solution)/shard_map/dot_general | solution.py:82
  25.2 23.2 %all-to-all-done.1 = bf16[8,2,32,1024]{3,2,1,0:T(8,128)(2,1)S(1)} async-done(((bf16[8,2,32,1024]{3,2,1,0:T(8,128)(2,1)}), bf16[8,2,32,1024]{3,2,1,0:T(8,128)(2,1)S(1)}, u32[]{:S(2)}, u32[]{:S(2)}) %all-to-all-start.1) | async-done | bytes 1048608 | tf_op jit(solution)/shard_map/all_to_all | solution.py:92
  48.4 4.2 %all-to-all-start = ((bf16[16,32,1024]{2,1,0:T(8,128)(2,1)}), bf16[16,32,1024]{2,1,0:T(8,128)(2,1)}, u32[]{:S(2)}, u32[]{:S(2)}) async-start(bf16[16,32,1024]{2,1,0:T(8,128)(2,1)} %bitcast.67), calls=%async_computation | async-start | bytes 2097152 | tf_op jit(solution)/shard_map/all_to_all | solution.py:90
  53.3 0.8 copy.39
  54.1 1.1 copy.41
  55.2 2.0 copy.40
  57.3 3.2 %fusion.29 = (f32[16,128]{1,0:T(8,128)S(1)}, f32[16,128,256]{2,1,0:T(8,128)}) fusion(pred[256]{0:T(512)(128)(4,1)S(1)} %iota_compare_fusion.5, bf16[128,16,64]{0,2,1:T(8,128)(2,1)} %bitcast.82, bf16[256,16,64]{0,2,1:T(8,128)(2,1)} %bitcast.80), kind=kOutput, calls=%fused_computation.52 | convolution fusion | flops 69206272 | bytes 2892032 | tf_op jit(solution)/shard_map/sub | solution.py:29
  60.4 2.2 convolution_convert_fusion.4
  62.6 0.8 fusion.30
  63.4 1.5 convolution_convert_fusion
  64.9 13.3 %all-to-all-done = bf16[16,32,1024]{2,1,0:T(8,128)(2,1)} async-done(((bf16[16,32,1024]{2,1,0:T(8,128)(2,1)}), bf16[16,32,1024]{2,1,0:T(8,128)(2,1)}, u32[]{:S(2)}, u32[]{:S(2)}) %all-to-all-start) | async-done | bytes 1048608 | tf_op jit(solution)/shard_map/all_to_all | solution.py:90
  78.2 3.7 %all-to-all-start.2 = ((bf16[16,32,1024]{2,1,0:T(8,128)(2,1)}), bf16[16,32,1024]{2,1,0:T(8,128)(2,1)S(1)}, u32[]{:S(2)}, u32[]{:S(2)}) async-start(bf16[16,32,1024]{2,1,0:T(8,128)(2,1)} %bitcast.25), calls=%async_computation.2 | async-start | bytes 2097152 | tf_op jit(solution)/shard_map/all_to_all | solution.py:100
  81.9 1.3 copy.43
  83.3 2.3 %copy.42 = bf16[8,2,32,1024]{3,2,0,1:T(8,128)(2,1)} copy(bf16[8,2,32,1024]{3,2,1,0:T(8,128)(2,1)} %bitcast.10) | data formatting | bytes 2097152 | tf_op jit(solution)/shard_map/all_to_all | solution.py:90
  85.6 22.1 %all-to-all-done.2 = bf16[16,32,1024]{2,1,0:T(8,128)(2,1)S(1)} async-done(((bf16[16,32,1024]{2,1,0:T(8,128)(2,1)}), bf16[16,32,1024]{2,1,0:T(8,128)(2,1)S(1)}, u32[]{:S(2)}, u32[]{:S(2)}) %all-to-all-start.2) | async-done | bytes 1048608 | tf_op jit(solution)/shard_map/all_to_all | solution.py:100
  107.7 1.1 copy.44
  108.7 10.4 %fusion.31 = f32[2,256,2816]{2,1,0:T(8,128)} fusion(bf16[2,256,1024]{2,1,0:T(8,128)(2,1)} %bitcast.70, bf16[2,1024,2816]{1,2,0:T(8,128)(2,1)} %all-gather.3.cloned.1.call-done), kind=kOutput, calls=%fused_computation.54 | convolution fusion | flops 2952790016 | bytes 18350080 | tf_op jit(solution)/shard_map/erd,edf->erf/dot_general | solution.py:43
  119.1 13.7 %fusion.32 = f32[2,256,2816]{2,1,0:T(8,128)} fusion(bf16[2,256,1024]{2,1,0:T(8,128)(2,1)S(1)} %bitcast.68, bf16[2,1024,2816]{1,2,0:T(8,128)(2,1)} %all-gather.3.cloned.1.call-done), kind=kOutput, calls=%fused_computation.55 | convolution fusion | flops 2952790016 | bytes 18350080 | tf_op jit(solution)/shard_map/erd,edf->erf/dot_general | solution.py:44
  132.9 32.6 %all-gather.5.cloned.1.call-done = bf16[2,1024,2816]{1,2,0:T(8,128)(2,1)} async-done(((bf16[2,1024,704]{1,2,0:T(8,128)(2,1)}), bf16[2,1024,2816]{1,2,0:T(8,128)(2,1)}) %all-gather.5.cloned.1.call-update) | async-done | bytes 11534352 | tf_op jit(solution)/shard_map/all_gather | solution.py:107
  165.5 15.6 %multiply_convert_fusion = bf16[2,256,2816]{2,1,0:T(8,128)(2,1)} fusion(f32[2,256,2816]{2,1,0:T(8,128)} %fusion.31, f32[2,256,2816]{2,1,0:T(8,128)} %fusion.32, bf16[2,256,1024]{2,1,0:T(8,128)(2,1)S(1)} %bitcast.69, bf16[2,1024,2816]{1,2,0:T(8,128)(2,1)} %all-gather.5.cloned.1.call-done), kind=kOutput, calls=%fused_computation.1 | convolution fusion | flops 2970091520 | bytes 27000832 | tf_op jit(solution)/shard_map/erd,edf->erf/dot_general | solution.py:45
  181.1 8.4 %convolution_convert_fusion.3 = bf16[2,256,1024]{2,1,0:T(8,128)(2,1)S(1)} fusion(bf16[2,256,2816]{2,1,0:T(8,128)(2,1)} %multiply_convert_fusion, bf16[2,1024,2816]{1,2,0:T(8,128)(2,1)} %all-gather.3.cloned.1.call-done), kind=kOutput, calls=%fused_computation.12 | convolution fusion | flops 2953314304 | bytes 15466496 | tf_op jit(solution)/shard_map/erf,edf->erd/dot_general | solution.py:49
  189.6 1.1 copy.45
  190.7 31.4 %all_to_all.56 = bf16[2,256,1024]{2,0,1:T(2,128)(2,1)S(1)} all-to-all(bf16[2,256,1024]{2,0,1:T(2,128)(2,1)S(1)} %copy.45), channel_id=1, replica_groups=mesh['expert'=8,'dp'=4] {'expert'}, dimensions={1} | all-to-all | bytes 2097152 | tf_op jit(solution)/shard_map/all_to_all | solution.py:109
  222.1 0.3 copy.46
  222.4 0.1 copy.47
  222.5 1.3 fusion.4
  223.8 0.0 copy-done.1
  (18 shorter events, 0.0 us)
Async XLA Ops:
  6.5 56.1 %copy-start = (bf16[1024,1024]{1,0:T(8,128)(2,1)S(1)}, bf16[1024,1024]{1,0:T(8,128)(2,1)}, u32[]{:S(2)}) copy-start(bf16[1024,1024]{1,0:T(8,128)(2,1)} %param.25) | copy-start | bytes 6291460
  6.5 1.5 copy-start.4
  6.5 1.7 copy-start.8
  6.5 1.7 copy-start.9
  6.5 1.7 copy-start.6
  6.5 102.2 %all-gather.3.cloned.1.call-start = ((), (), s32[]{:S(2)}) async-start(), calls=%async_computation.4 | async-start | bytes 14417920 | tf_op jit(solution)/shard_map/all_gather | solution.py:106
  7.3 158.2 %all-gather.5.cloned.1.call-start = ((), (), s32[]{:S(2)}) async-start(), calls=%async_computation.5 | async-start | bytes 14417920 | tf_op jit(solution)/shard_map/all_gather | solution.py:107
  8.3 45.0 %copy-start.5 = (bf16[1,1,128,1024]{3,2,1,0:T(8,128)(2,1)S(1)}, bf16[1,1,128,1024]{3,2,1,0:T(8,128)(2,1)}, u32[]{:S(2)}) copy-start(bf16[1,1,128,1024]{3,2,1,0:T(8,128)(2,1)} %param.16) | copy-start | bytes 786436
  15.3 33.0 %all-to-all-start.1 = ((bf16[8,2,32,1024]{3,2,1,0:T(8,128)(2,1)}), bf16[8,2,32,1024]{3,2,1,0:T(8,128)(2,1)S(1)}, u32[]{:S(2)}, u32[]{:S(2)}) async-start(bf16[8,2,32,1024]{3,2,1,0:T(8,128)(2,1)} %constant_dynamic-update-slice_fusion), calls=%async_computation.1 | async-start | bytes 2097152 | tf_op jit(solution)/shard_map/all_to_all | solution.py:92
  48.4 14.2 %copy-start.2 = (bf16[8,2,32,1024]{3,2,1,0:T(8,128)(2,1)}, bf16[8,2,32,1024]{3,2,1,0:T(8,128)(2,1)S(1)}, u32[]{:S(2)}) copy-start(bf16[8,2,32,1024]{3,2,1,0:T(8,128)(2,1)S(1)} %all-to-all-done.1) | copy-start | bytes 3145732
  48.4 29.8 %all-to-all-start = ((bf16[16,32,1024]{2,1,0:T(8,128)(2,1)}), bf16[16,32,1024]{2,1,0:T(8,128)(2,1)}, u32[]{:S(2)}, u32[]{:S(2)}) async-start(bf16[16,32,1024]{2,1,0:T(8,128)(2,1)} %bitcast.67), calls=%async_computation | async-start | bytes 2097152 | tf_op jit(solution)/shard_map/all_to_all | solution.py:90
  60.4 3.0 %copy-start.7 = (f32[1,1,256]{2,1,0:T(1,128)S(1)}, f32[1,1,256]{2,1,0:T(1,128)}, u32[]{:S(2)}) copy-start(f32[1,1,256]{2,1,0:T(1,128)} %param.21) | copy-start | bytes 3076
  78.2 29.5 %all-to-all-start.2 = ((bf16[16,32,1024]{2,1,0:T(8,128)(2,1)}), bf16[16,32,1024]{2,1,0:T(8,128)(2,1)S(1)}, u32[]{:S(2)}, u32[]{:S(2)}) async-start(bf16[16,32,1024]{2,1,0:T(8,128)(2,1)} %bitcast.25), calls=%async_computation.2 | async-start | bytes 2097152 | tf_op jit(solution)/shard_map/all_to_all | solution.py:100
  119.1 46.4 %copy-start.3 = (bf16[2,8,32,1024]{3,2,1,0:T(8,128)(2,1)S(1)}, bf16[2,8,32,1024]{3,2,1,0:T(8,128)(2,1)}, u32[]{:S(2)}) copy-start(bf16[2,8,32,1024]{3,2,1,0:T(8,128)(2,1)} %copy.44) | copy-start | bytes 3145732
  181.1 42.6 %copy-start.1 = (bf16[1024,1024]{1,0:T(8,128)(2,1)S(1)}, bf16[1024,1024]{1,0:T(8,128)(2,1)}, u32[]{:S(2)}) copy-start(bf16[1024,1024]{1,0:T(8,128)(2,1)} %param.25) | copy-start | bytes 6291460
Sparse Core Ops, SparseCore 0:
  8.9 78.8 all-gather.2
  89.4 76.1 all-gather.4
